TPU v7x, 32 devices: a whole 2x2x4 slice. The times are simulated.
32 devices in a mesh: grp: 4 (over y, core), span: 8 (over z, x).
Axes of the slice: x: 2, y: 2, z: 4, core: 2. Of those that a mesh axis runs over, the one named last changes fastest.
Arguments:
- record: float32 [131072, 128], P(('grp', 'span')), may hold values from -96 to 96, as said below
Outputs:
- triangle: float32 [512, 512], replicated
- operator: float32 [512, 512], replicated
Inputs may be any that keep to these rules, and one draw needn't show every extreme that they name: `record`: Real-valued probe samples.
All inputs are finite; a program needn't handle non-finite values.
Results may differ from a plain program's by a relative error of at most 0.0003.
Values sent between devices are 32-bit elements; how exact they have to be, the bound alone decides.
A program may use at most 64 MiB of HBM per device.

v0:
```python
import functools

import jax
import jax.numpy as jnp
from jax import lax
from jax.experimental import pallas as pl
from jax.experimental.pallas import tpu as pltpu
from jax.sharding import PartitionSpec as P

LAGS = 4
DELAY = 1024
AXES = ("grp", "span")
HIGH = lax.Precision.HIGHEST
MESH = pl.DeviceIdType.MESH
UNIT = 128
HALF = DELAY // 2
CHUNKS = HALF // UNIT
GRAM = [(k, l) for k in range(LAGS) for l in range(k, LAGS)]
CROSS = [(k, l) for k in range(LAGS) for l in range(LAGS)]
NB = len(GRAM) + len(CROSS)


def contract(left, right, dims, precision=None):
    return lax.dot_general(
        left, right, (dims, ((), ())), precision=precision,
        preferred_element_type=jnp.float32,
    )


def factor(block):
    n = block.shape[0]
    groups = n // 8
    lane = lax.broadcasted_iota(jnp.int32, (8, n), 1)
    sub = lax.broadcasted_iota(jnp.int32, (8, n), 0)
    a = [block[8 * g:8 * g + 8, :] for g in range(groups)]
    b = [jnp.where(lane == sub + 8 * g, 1.0, 0.0) for g in range(groups)]
    for k in range(n):
        g, r = divmod(k, 8)
        inverse = 1.0 / a[g][r:r + 1, k:k + 1]
        row = a[g][r:r + 1, :] * inverse
        brow = b[g][r:r + 1, :] * inverse
        for h in range(g, groups):
            if h == g and r == 7:
                continue
            column = jnp.broadcast_to(a[h][:, k:k + 1], (8, n))
            if h == g:
                column = jnp.where(sub > r, column, 0.0)
            a[h] = a[h] - column * row
            b[h] = b[h] - column * brow
    for g in range(groups):
        here = lane == sub + 8 * g
        pivot = jnp.sum(jnp.where(here, a[g], 0.0), axis=1, keepdims=True)
        scale = 1.0 / jnp.sqrt(pivot)
        a[g] = jnp.where(lane >= sub + 8 * g, a[g] * scale, 0.0)
        b[g] = b[g] * scale
    return jnp.concatenate(a, 0), jnp.concatenate(b, 0)


def solve_kernel(comps, scale, sums_ref, tri_ref, op_ref, work, inverses):
    size = LAGS * comps
    for i in range(LAGS):
        rows = pl.ds(i * comps, comps)
        for j in range(LAGS):
            if j >= i:
                at = GRAM.index((i, j)) * comps
                work[i, :, pl.ds(j * comps, comps)] = sums_ref[pl.ds(at, comps), :] * scale
            at = (len(GRAM) + CROSS.index((i, j))) * comps
            work[i, :, pl.ds(size + j * comps, comps)] = sums_ref[pl.ds(at, comps), :] * scale
        if i:
            work[i, :, pl.ds(0, i * comps)] = jnp.zeros((comps, i * comps), jnp.float32)
            tri_ref[rows, pl.ds(0, i * comps)] = jnp.zeros((comps, i * comps), jnp.float32)

    def step(i, carry):
        at = pl.multiple_of(i * comps, comps)
        upper, inverse = factor(work[i, :, pl.ds(at, comps)])
        inverses[i] = inverse
        work[i] = contract(inverse, work[i], ((1,), (0,)), HIGH)
        work[i, :, pl.ds(at, comps)] = upper

        def update(j, carry):
            to = pl.multiple_of(j * comps, comps)
            work[j] = work[j] - contract(work[i, :, pl.ds(to, comps)], work[i], ((0,), (0,)), HIGH)
            return carry
        lax.fori_loop(i + 1, LAGS, update, 0)
        return carry
    lax.fori_loop(0, LAGS, step, 0)

    for i in range(LAGS):
        for j in range(i, LAGS):
            tri_ref[pl.ds(i * comps, comps), pl.ds(j * comps, comps)] = work[i, :, pl.ds(j * comps, comps)]
    for b in range(LAGS):
        rest = jnp.concatenate(
            [work[i, :, pl.ds((LAGS + b) * comps, comps)] for i in range(LAGS)], 0)
        if b:
            rest = rest - contract(
                op_ref[:, pl.ds(0, b * comps)],
                tri_ref[pl.ds(0, b * comps), pl.ds(b * comps, comps)], ((1,), (0,)), HIGH)
        op_ref[:, pl.ds(b * comps, comps)] = contract(rest, inverses[b], ((1,), (1,)), HIGH)


def halves(x):
    spread = x * 65537.0
    high = spread - (spread - x)
    return high.astype(jnp.bfloat16), (x - high).astype(jnp.bfloat16)


def quarters(x):
    n = x.shape[0] // 2
    return (x[:n, :n] + x[:n, n:]) + (x[n:, :n] + x[n:, n:])


def prepare(window, at, left, right, after):
    cols = pl.ds(at, UNIT)
    rows = window[:UNIT]
    high, low = halves(rows)
    right[cols, pl.ds(0, UNIT)] = high
    right[cols, pl.ds(UNIT, UNIT)] = low
    high, low = halves(rows.T)
    left[pl.ds(0, UNIT), cols] = high
    left[pl.ds(UNIT, UNIT), cols] = low
    high, low = halves(pltpu.roll(window, window.shape[0] - 1, 0)[:UNIT])
    after[cols, pl.ds(0, UNIT)] = high
    after[cols, pl.ds(UNIT, UNIT)] = low


def product(left, lcol, right, rrow, depth):
    lcol = pl.multiple_of(lcol, UNIT)
    rrow = pl.multiple_of(rrow, UNIT)
    return jnp.dot(left[:, pl.ds(lcol, depth)], right[pl.ds(rrow, depth), :],
                   preferred_element_type=jnp.float32)


def sums_kernel(groups, spans, piece, rec, out, ext, own, left, right, after, acc,
                eleft, eright, eafter, dgram, dcross, wgram, wcross, buf, slot_a, slot_b, slot_c,
                local_sem, xs, xr, zs, zr, es, er, as_, ar, bs, br, cs, cr, gcs, gcr, gbs, gbr, gas, gar):
    grp, span = lax.axis_index("grp"), lax.axis_index("span")
    pairs = spans // 2
    h, q = span % 2, span // 2
    core, y = grp % 2, grp // 2
    plane, place = groups, y * 2 + h
    at, count = grp * pairs + q, groups * pairs
    has_prev, has_next = at > 0, at < count - 1

    def device(pair, side):
        pair = (pair + count) % count
        return (pair // pairs, (pair % pairs) * 2 + side)

    def plane_peer(d):
        there = (place + d) % plane
        return ((there // 2) * 2 + core, q * 2 + there % 2)

    def line_peer(d):
        return (grp, ((q + d) % pairs) * 2 + h)

    core_peer = (y * 2 + 1 - core, span)
    partner = (grp, q * 2 + 1 - h)
    z_to = device(at - 1 + 2 * h, h)
    sends_z = jnp.where(h == 0, at, count - 1 - at) > 0
    gets_z = jnp.where(h == 0, count - 1 - at, at) > 0

    own_copy = pltpu.make_async_copy(
        rec.at[:, pl.ds(h * HALF, HALF), :], ext.at[pl.ds(1 + 7 * h, 4), pl.ds(0, HALF), :], local_sem.at[0])
    own_extra = pltpu.make_async_copy(
        rec.at[:, pl.ds((1 - h) * HALF, 8), :], ext.at[pl.ds(1 + 6 * h, 4), pl.ds(HALF, 8), :], local_sem.at[1])
    own_copy.start()
    own_extra.start()
    edge = (at * 2 + h == 0) | (at * 2 + h == 2 * count - 1)
    full_copy = pltpu.make_async_copy(rec, own.at[pl.ds(0, LAGS)], local_sem.at[2])

    @pl.when(edge)
    def _():
        full_copy.start()

    barrier = pltpu.get_barrier_semaphore()

    def greet(to):
        pl.semaphore_signal(barrier, inc=1, device_id=to, device_id_type=MESH)

    greet(core_peer)
    for d in range(1, plane):
        greet(plane_peer(d))
    for d in range(1, pairs):
        greet(line_peer(d))

    @pl.when(has_prev)
    def _():
        greet(device(at - 1, h))

    @pl.when(has_next)
    def _():
        greet(device(at + 1, h))

    @pl.when((h == 0) & has_prev)
    def _():
        greet(device(at - 1, 1))

    @pl.when((h == 1) & has_next)
    def _():
        greet(device(at + 1, 0))

    pl.semaphore_wait(
        barrier, plane + pairs - 1
        + jnp.where(has_prev, 1, 0) + jnp.where(has_next, 1, 0)
        + jnp.where((h == 0) & has_prev, 1, 0) + jnp.where((h == 1) & has_next, 1, 0))

    def remote(src, dst, send, recv, to):
        return pltpu.make_async_remote_copy(
            src_ref=src, dst_ref=dst, send_sem=send, recv_sem=recv, device_id=to, device_id_type=MESH)

    def x_copy(c):
        return remote(
            rec.at[:, pl.ds((1 - h) * HALF + c * UNIT, UNIT), :],
            ext.at[pl.ds(4 + h, 4), pl.ds(c * UNIT, UNIT), :], xs.at[c], xr.at[c], partner)

    def z_copy(c):
        return remote(
            rec.at[pl.ds(h, 3), pl.ds(h * HALF + c * UNIT, UNIT), :],
            ext.at[pl.ds(9 - 8 * h, 3), pl.ds(c * UNIT, UNIT), :], zs.at[c], zr.at[c], z_to)

    x_extra = remote(
        rec.at[:, pl.ds(h * HALF, 8), :], ext.at[pl.ds(3 + 2 * h, 4), pl.ds(HALF, 8), :],
        es.at[0], er.at[0], partner)
    z_extra = remote(
        rec.at[pl.ds(h, 3), pl.ds((1 - h) * HALF, 8), :], ext.at[pl.ds(9 - 9 * h, 3), pl.ds(HALF, 8), :],
        es.at[1], er.at[1], z_to)
    d_extra = remote(
        rec.at[pl.ds(0, 1), pl.ds(0, 8), :], ext.at[pl.ds(11, 1), pl.ds(HALF, 8), :],
        es.at[2], er.at[2], device(at - 1, 1))

    x_extra.start()
    for c in reversed(range(CHUNKS)):
        x_copy(c).start()

    @pl.when(sends_z)
    def _():
        z_extra.start()
        for c in reversed(range(CHUNKS)):
            z_copy(c).start()

    @pl.when((h == 0) & has_prev)
    def _():
        d_extra.start()

    @pl.when(jnp.logical_not(gets_z))
    def _():
        ext[pl.ds(9 - 8 * h, 3), pl.ds(0, HALF), :] = jnp.zeros((3, HALF, UNIT), jnp.float32)

    acc[...] = jnp.zeros(acc.shape, jnp.float32)

    @pl.when(edge)
    def _():
        last = jnp.where(at > 0, 1, 0)
        own[LAGS, pl.ds(0, 8), :] = jnp.zeros((8, UNIT), jnp.float32)
        full_copy.wait()
        parts = DELAY // UNIT

        def unit(t, carry):
            block, row = t // parts, (t % parts) * UNIT
            rows = own[last + block, pl.ds(pl.multiple_of(row, UNIT), UNIT), :]
            more = t + 1
            tail = own[last + more // parts, pl.ds(pl.multiple_of((more % parts) * UNIT, UNIT), 8), :]
            prepare(jnp.concatenate([rows, tail], 0), pl.multiple_of(t * UNIT, UNIT), eleft, eright, eafter)
            return carry
        lax.fori_loop(0, 3 * parts, unit, 0)

        def excess(t, carry):
            i, j = t // 3, t % 3
            dgram[t] = quarters(product(eleft, i * DELAY, eright, j * DELAY, DELAY))
            dcross[t] = quarters(product(eleft, i * DELAY, eafter, j * DELAY, DELAY))
            return carry
        lax.fori_loop(0, 9, excess, 0)

        sub = lax.broadcasted_iota(jnp.int32, (8, UNIT), 0)

        def pick(block, start, row):
            rows = jnp.where(sub == row, own[block, pl.ds(pl.multiple_of(start, 8), 8), :], 0.0)
            line = jnp.sum(rows, axis=0, keepdims=True)
            return jnp.where(sub == 0, jnp.broadcast_to(line, (8, UNIT)), 0.0)
        ends = jnp.concatenate([pick(k, last * (DELAY - 8), last * 7) for k in range(LAGS)], 1)
        lead = jnp.concatenate([pick(l + 1, 0, 0) for l in range(LAGS)], 1)
        lead = lead * last.astype(jnp.float32)
        wgram[...] = (0.5 + last.astype(jnp.float32)) * contract(ends, ends, ((0,), (0,)), HIGH)
        wcross[...] = contract(ends, lead, ((0,), (0,)), HIGH)

    own_copy.wait()
    own_extra.wait()
    x_extra.wait_recv()

    @pl.when(gets_z)
    def _():
        z_extra.wait_recv()

    @pl.when((h == 1) & has_next)
    def _():
        d_extra.wait_recv()

    @pl.when((h == 0) & jnp.logical_not(has_next))
    def _():
        ext[pl.ds(9, 3), pl.ds(HALF, 8), :] = jnp.zeros((3, 8, UNIT), jnp.float32)

    @pl.when((h == 1) & jnp.logical_not(has_prev))
    def _():
        ext[pl.ds(0, 4), pl.ds(HALF, 8), :] = jnp.zeros((4, 8, UNIT), jnp.float32)

    @pl.when((h == 1) & jnp.logical_not(has_next))
    def _():
        ext[pl.ds(11, 1), pl.ds(HALF, 8), :] = jnp.zeros((1, 8, UNIT), jnp.float32)

    def chunk(step, carry):
        c = CHUNKS - 1 - step
        x_copy(c).wait_recv()

        @pl.when(gets_z)
        def _():
            z_copy(c).wait_recv()

        def unit(e, carry):
            prepare(ext[e + 1, pl.ds(pl.multiple_of(c * UNIT, UNIT), UNIT + 8), :],
                    pl.multiple_of(e * UNIT, UNIT), left, right, after)
            return carry
        lax.fori_loop(0, 11, unit, 0)

        def lag(p, carry):
            a = h * (3 - p) * UNIT
            b = a + p * UNIT
            acc[p] += product(left, a, right, b, 8 * UNIT)
            acc[LAGS + p] += product(left, a, after, b, 8 * UNIT)
            acc[2 * LAGS + p] += product(left, b, after, a, 8 * UNIT)
            return carry
        lax.fori_loop(0, LAGS, lag, 0)
        return carry
    lax.fori_loop(0, CHUNKS, chunk, 0)

    def term(n, k, l):
        if n < len(GRAM):
            return quarters(acc[l - k])
        return quarters(acc[LAGS + l - k] if l >= k else acc[2 * LAGS + k - l])

    blocks = GRAM + CROSS

    @pl.when(jnp.logical_not(edge))
    def _():
        for m in range(-LAGS + 1, LAGS):
            for first in (True, False):
                which = [n for n, (k, l) in enumerate(blocks) if l - k == m and (n < len(GRAM)) == first]
                if which:
                    value = term(which[0], *blocks[which[0]])
                    for n in which:
                        buf[pl.ds(n * UNIT, UNIT), :] = value

    @pl.when(edge)
    def _():
        last = jnp.where(at > 0, 1, 0).astype(jnp.float32)
        for n, (k, l) in enumerate(blocks):
            m = l - k
            value = term(n, k, l)
            less, ends = (dgram, wgram) if n < len(GRAM) else (dcross, wcross)
            for i in range(max(0, -m), min(2, 2 - m) + 1):
                value = value - less[3 * i + i + m] * ((1.0 - last) if i < k else last)
            value = value - ends[pl.ds(k * UNIT, UNIT), pl.ds(l * UNIT, UNIT)]
            buf[pl.ds(n * UNIT, UNIT), :] = value

    total = 2 * plane * pairs * piece
    if total > NB * UNIT:
        buf[pl.ds(NB * UNIT, total - NB * UNIT), :] = jnp.zeros((total - NB * UNIT, UNIT), jnp.float32)

    def rows(n, size, base=0):
        return pl.ds(pl.multiple_of(base + n * size, 8), size)

    part = plane * pairs * piece
    copy = remote(buf.at[rows(1 - core, part)], slot_a, as_.at[0], ar.at[0], core_peer)
    copy.start()
    copy.wait()
    base_a = core * part
    buf[rows(core, part), :] += slot_a[...]
    sub_part = pairs * piece
    copies = []
    for d in range(1, plane):
        there = (place + d) % plane
        copies.append(remote(buf.at[rows(there, sub_part, base_a)], slot_b.at[d - 1],
                             bs.at[d - 1], br.at[d - 1], plane_peer(d)))
        copies[-1].start()
    for c in copies:
        c.wait()
    base_b = base_a + place * sub_part
    value = buf[rows(0, sub_part, base_b), :]
    for d in range(1, plane):
        value = value + slot_b[d - 1]
    buf[rows(0, sub_part, base_b), :] = value
    copies = []
    for d in range(1, pairs):
        there = (q + d) % pairs
        copies.append(remote(buf.at[rows(there, piece, base_b)], slot_c.at[d - 1],
                             cs.at[d - 1], cr.at[d - 1], line_peer(d)))
        copies[-1].start()
    for c in copies:
        c.wait()
    base_c = base_b + q * piece
    value = buf[rows(0, piece, base_c), :]
    for d in range(1, pairs):
        value = value + slot_c[d - 1]
    mine = out.at[rows(0, piece, base_c)]
    out[rows(0, piece, base_c), :] = value

    copies = []
    for d in range(1, pairs):
        copies.append(remote(mine, mine, gcs.at[d - 1], gcr.at[d - 1], line_peer(d)))
        copies[-1].start()
    for c in copies:
        c.wait()
    mine = out.at[rows(0, sub_part, base_b)]
    copies = []
    for d in range(1, plane):
        copies.append(remote(mine, mine, gbs.at[d - 1], gbr.at[d - 1], plane_peer(d)))
        copies[-1].start()
    for c in copies:
        c.wait()
    mine = out.at[rows(0, part, base_a)]
    copy = remote(mine, mine, gas.at[0], gar.at[0], core_peer)
    copy.start()
    copy.wait()

    x_extra.wait_send()
    for c in range(CHUNKS):
        x_copy(c).wait_send()

    @pl.when(sends_z)
    def _():
        z_extra.wait_send()
        for c in range(CHUNKS):
            z_copy(c).wait_send()

    @pl.when((h == 0) & has_prev)
    def _():
        d_extra.wait_send()


def on_device(record):
    count, comps = record.shape
    groups, spans = lax.axis_size("grp"), lax.axis_size("span")
    devices = groups * spans
    lead = (LAGS - 1) * DELAY + 1
    last_row = count * devices - lead
    pairs = spans // 2
    piece = -(-NB * UNIT // (devices * 8)) * 8
    total = piece * devices
    dma = pltpu.SemaphoreType.DMA
    f32, bf16 = jnp.float32, jnp.bfloat16
    vmem = pl.BlockSpec(memory_space=pltpu.VMEM)
    sums = pl.pallas_call(
        functools.partial(sums_kernel, groups, spans, piece),
        out_shape=jax.ShapeDtypeStruct((total, comps), f32),
        in_specs=[pl.BlockSpec(memory_space=pl.ANY)], out_specs=vmem,
        scratch_shapes=[
            pltpu.VMEM((12, HALF + 8, UNIT), f32),
            pltpu.VMEM((LAGS + 1, DELAY, UNIT), f32),
            pltpu.VMEM((2 * UNIT, 11 * UNIT), bf16),
            pltpu.VMEM((11 * UNIT, 2 * UNIT), bf16),
            pltpu.VMEM((11 * UNIT, 2 * UNIT), bf16),
            pltpu.VMEM((3 * LAGS, 2 * UNIT, 2 * UNIT), f32),
            pltpu.VMEM((2 * UNIT, 3 * DELAY), bf16),
            pltpu.VMEM((3 * DELAY, 2 * UNIT), bf16),
            pltpu.VMEM((3 * DELAY, 2 * UNIT), bf16),
            pltpu.VMEM((9, UNIT, UNIT), f32),
            pltpu.VMEM((9, UNIT, UNIT), f32),
            pltpu.VMEM((LAGS * UNIT, LAGS * UNIT), f32),
            pltpu.VMEM((LAGS * UNIT, LAGS * UNIT), f32),
            pltpu.VMEM((total, UNIT), f32),
            pltpu.VMEM((total // 2, UNIT), f32),
            pltpu.VMEM((groups - 1, pairs * piece, UNIT), f32),
            pltpu.VMEM((pairs - 1, piece, UNIT), f32),
            dma((3,)), dma((CHUNKS,)), dma((CHUNKS,)), dma((CHUNKS,)), dma((CHUNKS,)), dma((3,)), dma((3,)),
            dma((1,)), dma((1,)), dma((groups - 1,)), dma((groups - 1,)), dma((pairs - 1,)), dma((pairs - 1,)),
            dma((pairs - 1,)), dma((pairs - 1,)), dma((groups - 1,)), dma((groups - 1,)), dma((1,)), dma((1,)),
        ],
        compiler_params=pltpu.CompilerParams(
            collective_id=0, has_side_effects=True, vmem_limit_bytes=56 << 20),
    )(record.reshape(LAGS, DELAY, comps))
    size = LAGS * comps
    return pl.pallas_call(
        functools.partial(solve_kernel, comps, 1.0 / last_row),
        out_shape=(jax.ShapeDtypeStruct((size, size), f32),) * 2,
        in_specs=[vmem], out_specs=(vmem, vmem),
        scratch_shapes=[
            pltpu.VMEM((LAGS, comps, 2 * size), f32),
            pltpu.VMEM((LAGS, comps, comps), f32),
        ],
        compiler_params=pltpu.CompilerParams(vmem_limit_bytes=48 << 20),
    )(sums)


def solution(mesh):
    placed = (P(AXES, None),)
    return jax.shard_map(
        on_device, mesh=mesh, in_specs=placed, out_specs=(P(), P()), check_vma=False
    )
```

profile of v0, /device:TPU:0, one launch (start us, length us, event | category | flops | bytes accessed | tf_op | source)
XLA Modules:
  0.0 133.1 jit_solution(426806019417607597)
XLA Ops:
  0.6 76.5 %shard_map.30.sums_ref = f32[3328,128]{1,0:T(8,128)} custom-call(f32[4,1024,128]{2,1,0:T(8,128)} %bitcast.1), custom_call_target="tpu_custom_call" | custom-call | tf_op jit(solution)/shard_map/pallas_call | solution.py:450
  77.1 0.0 copy-start
  77.1 1.4 %copy-done = f32[3328,128]{1,0:T(8,128)S(1)} copy-done((f32[3328,128]{1,0:T(8,128)S(1)}, f32[3328,128]{1,0:T(8,128)}, u32[]{:S(2)}) %copy-start) | copy-done | bytes 1703960
  78.6 54.5 %shard_map.31 = (f32[512,512]{1,0:T(8,128)}, f32[512,512]{1,0:T(8,128)}) custom-call(f32[3328,128]{1,0:T(8,128)S(1)} %copy-done), custom_call_target="tpu_custom_call" | custom-call | tf_op jit(solution)/shard_map/pallas_call | solution.py:480
Async XLA Ops:
  77.1 1.5 %copy-start = (f32[3328,128]{1,0:T(8,128)S(1)}, f32[3328,128]{1,0:T(8,128)}, u32[]{:S(2)}) copy-start(f32[3328,128]{1,0:T(8,128)} %shard_map.30.sums_ref) | copy-start | bytes 5111812
where the time goes:
time: 135 us; the launch traced here: 133 us
  Pallas kernels  131 us (97%)
  local copies, waits for them, and re-layouts  1.45 us (1%)
    pallas_call x1, Pallas kernels, on_device(): pl.pallas_call(functools.partial(sums_kernel, groups, spans, piece), out_...  76.5 us
    pallas_call x1, Pallas kernels, on_device(): pl.pallas_call(functools.partial(solve_kernel, comps, 1.0 / last_row), ou...  54.5 us

commit v1 on v0

--- a/solution.py
+++ b/solution.py
@@ -34,38 +34,64 @@
     sub = lax.broadcasted_iota(jnp.int32, (8, n), 0)
     a = [block[8 * g:8 * g + 8, :] for g in range(groups)]
     b = [jnp.where(lane == sub + 8 * g, 1.0, 0.0) for g in range(groups)]
-    for k in range(n):
-        g, r = divmod(k, 8)
-        inverse = 1.0 / a[g][r:r + 1, k:k + 1]
-        row = a[g][r:r + 1, :] * inverse
-        brow = b[g][r:r + 1, :] * inverse
-        for h in range(g, groups):
-            if h == g and r == 7:
-                continue
-            column = jnp.broadcast_to(a[h][:, k:k + 1], (8, n))
-            if h == g:
-                column = jnp.where(sub > r, column, 0.0)
-            a[h] = a[h] - column * row
-            b[h] = b[h] - column * brow
+
+    def column(x, k):
+        return jnp.broadcast_to(x[:, k:k + 1], (8, n))
+
+    def line(x, i):
+        return jnp.broadcast_to(x[i:i + 1, :], (8, n))
+
+    def stack(rows):
+        value = rows[0]
+        for i in range(1, 8):
+            value = jnp.where(sub == i, rows[i], value)
+        return value
+
     for g in range(groups):
-        here = lane == sub + 8 * g
-        pivot = jnp.sum(jnp.where(here, a[g], 0.0), axis=1, keepdims=True)
-        scale = 1.0 / jnp.sqrt(pivot)
-        a[g] = jnp.where(lane >= sub + 8 * g, a[g] * scale, 0.0)
-        b[g] = b[g] * scale
+        cols = [column(a[g], 8 * g + j) for j in range(8)]
+        s = [[line(cols[j], i) for j in range(i + 1)] for i in range(8)]
+        rows = [line(a[g], i) for i in range(8)]
+        lines = [line(b[g], i) for i in range(8)]
+        inverse = []
+        for r in range(8):
+            inverse.append(1.0 / s[r][r])
+            factors = [s[i][r] * inverse[r] for i in range(r + 1, 8)]
+            for i in range(r + 1, 8):
+                for j in range(r + 1, i + 1):
+                    s[i][j] = s[i][j] - factors[i - r - 1] * s[j][r]
+            for i in range(r + 1, 8):
+                s[i][r] = factors[i - r - 1]
+                rows[i] = rows[i] - s[i][r] * rows[r]
+                lines[i] = lines[i] - s[i][r] * lines[r]
+        scale = lax.rsqrt(stack([s[r][r] for r in range(8)]))
+        left, right = list(rows), list(lines)
+        for r in reversed(range(8)):
+            left[r] = rows[r] * inverse[r]
+            right[r] = lines[r] * inverse[r]
+            for i in range(r + 1, 8):
+                left[r] = left[r] - s[i][r] * left[i]
+                right[r] = right[r] - s[i][r] * right[i]
+        for h in range(g + 1, groups):
+            old = a[h]
+            for j in range(8):
+                c = column(old, 8 * g + j)
+                a[h] = a[h] - c * left[j]
+                b[h] = b[h] - c * right[j]
+        a[g] = jnp.where(lane >= sub + 8 * g, stack(rows) * scale, 0.0)
+        b[g] = stack(lines) * scale
     return jnp.concatenate(a, 0), jnp.concatenate(b, 0)
 
 
-def solve_kernel(comps, scale, sums_ref, tri_ref, op_ref, work, inverses):
+def solve_kernel(comps, scale, gram_ref, cross_ref, tri_ref, op_ref, work, inverses):
     size = LAGS * comps
     for i in range(LAGS):
         rows = pl.ds(i * comps, comps)
         for j in range(LAGS):
             if j >= i:
                 at = GRAM.index((i, j)) * comps
-                work[i, :, pl.ds(j * comps, comps)] = sums_ref[pl.ds(at, comps), :] * scale
-            at = (len(GRAM) + CROSS.index((i, j))) * comps
-            work[i, :, pl.ds(size + j * comps, comps)] = sums_ref[pl.ds(at, comps), :] * scale
+                work[i, :, pl.ds(j * comps, comps)] = gram_ref[pl.ds(at, comps), :] * scale
+            at = CROSS.index((i, j)) * comps
+            work[i, :, pl.ds(size + j * comps, comps)] = cross_ref[pl.ds(at, comps), :] * scale
         if i:
             work[i, :, pl.ds(0, i * comps)] = jnp.zeros((comps, i * comps), jnp.float32)
             tri_ref[rows, pl.ds(0, i * comps)] = jnp.zeros((comps, i * comps), jnp.float32)
@@ -130,9 +156,59 @@
                    preferred_element_type=jnp.float32)
 
 
-def sums_kernel(groups, spans, piece, rec, out, ext, own, left, right, after, acc,
-                eleft, eright, eafter, dgram, dcross, wgram, wcross, buf, slot_a, slot_b, slot_c,
-                local_sem, xs, xr, zs, zr, es, er, as_, ar, bs, br, cs, cr, gcs, gcr, gbs, gbr, gas, gar):
+class Total:
+    def __init__(self, remote, core, place, q, plane, pairs, piece, peers, refs):
+        self.buf, self.out, self.slots = refs[0], refs[1], refs[2:5]
+        self.sems = refs[5:]
+        self.remote, self.piece = remote, piece
+        self.sizes = (plane * pairs * piece, pairs * piece, piece)
+        self.index, self.counts, self.peers = (core, place, q), (2, plane, pairs), peers
+        self.base = [0]
+        for size, index in zip(self.sizes, self.index):
+            self.base.append(self.base[-1] + index * size)
+        self.copies = []
+
+    def rows(self, level, n):
+        size = self.sizes[level]
+        return pl.ds(pl.multiple_of(self.base[level] + n * size, 8), size)
+
+    def send(self, level):
+        self.copies = []
+        for d in range(1, self.counts[level]):
+            there = (self.index[level] + d) % self.counts[level]
+            self.copies.append(self.remote(
+                self.buf.at[self.rows(level, there)], self.slots[level].at[d - 1],
+                self.sems[0].at[level, d - 1], self.sems[1].at[level, d - 1], self.peers[level](d)))
+            self.copies[-1].start()
+
+    def add(self, level):
+        for copy in self.copies:
+            copy.wait()
+        mine = self.rows(level, self.index[level])
+        value = self.buf[mine, :]
+        for d in range(1, self.counts[level]):
+            value = value + self.slots[level][d - 1]
+        if level == 2:
+            self.out[mine, :] = value
+        else:
+            self.buf[mine, :] = value
+
+    def share(self, level):
+        mine = self.out.at[self.rows(level, self.index[level])]
+        self.copies = []
+        for d in range(1, self.counts[level]):
+            self.copies.append(self.remote(
+                mine, mine, self.sems[2].at[level, d - 1], self.sems[3].at[level, d - 1], self.peers[level](d)))
+            self.copies[-1].start()
+
+    def wait(self):
+        for copy in self.copies:
+            copy.wait()
+
+
+def sums_kernel(groups, spans, pieces, rec, gram_out, cross_out, ext, own, left, right, after, acc,
+                eleft, eright, eafter, dgram, dcross, wgram, wcross,
+                local_sem, xs, xr, zs, zr, es, er, *reduce_refs):
     grp, span = lax.axis_index("grp"), lax.axis_index("span")
     pairs = spans // 2
     h, q = span % 2, span // 2
@@ -337,88 +413,64 @@
         return quarters(acc[LAGS + l - k] if l >= k else acc[2 * LAGS + k - l])
 
     blocks = GRAM + CROSS
-
-    @pl.when(jnp.logical_not(edge))
-    def _():
-        for m in range(-LAGS + 1, LAGS):
-            for first in (True, False):
-                which = [n for n, (k, l) in enumerate(blocks) if l - k == m and (n < len(GRAM)) == first]
+    half = len(reduce_refs) // 2
+    peers = (lambda d: core_peer, plane_peer, line_peer)
+    gram, cross = (
+        Total(remote, core, place, q, plane, pairs, piece, peers, (refs[0], out) + refs[1:])
+        for piece, out, refs in zip(pieces, (gram_out, cross_out), (reduce_refs[:half], reduce_refs[half:])))
+
+    def gather(total, numbers):
+        @pl.when(jnp.logical_not(edge))
+        def _():
+            for m in range(-LAGS + 1, LAGS):
+                which = [n for n in numbers if blocks[n][1] - blocks[n][0] == m]
                 if which:
                     value = term(which[0], *blocks[which[0]])
                     for n in which:
-                        buf[pl.ds(n * UNIT, UNIT), :] = value
-
-    @pl.when(edge)
-    def _():
-        last = jnp.where(at > 0, 1, 0).astype(jnp.float32)
-        for n, (k, l) in enumerate(blocks):
-            m = l - k
-            value = term(n, k, l)
-            less, ends = (dgram, wgram) if n < len(GRAM) else (dcross, wcross)
-            for i in range(max(0, -m), min(2, 2 - m) + 1):
-                value = value - less[3 * i + i + m] * ((1.0 - last) if i < k else last)
-            value = value - ends[pl.ds(k * UNIT, UNIT), pl.ds(l * UNIT, UNIT)]
-            buf[pl.ds(n * UNIT, UNIT), :] = value
-
-    total = 2 * plane * pairs * piece
-    if total > NB * UNIT:
-        buf[pl.ds(NB * UNIT, total - NB * UNIT), :] = jnp.zeros((total - NB * UNIT, UNIT), jnp.float32)
-
-    def rows(n, size, base=0):
-        return pl.ds(pl.multiple_of(base + n * size, 8), size)
-
-    part = plane * pairs * piece
-    copy = remote(buf.at[rows(1 - core, part)], slot_a, as_.at[0], ar.at[0], core_peer)
-    copy.start()
-    copy.wait()
-    base_a = core * part
-    buf[rows(core, part), :] += slot_a[...]
-    sub_part = pairs * piece
-    copies = []
-    for d in range(1, plane):
-        there = (place + d) % plane
-        copies.append(remote(buf.at[rows(there, sub_part, base_a)], slot_b.at[d - 1],
-                             bs.at[d - 1], br.at[d - 1], plane_peer(d)))
-        copies[-1].start()
-    for c in copies:
-        c.wait()
-    base_b = base_a + place * sub_part
-    value = buf[rows(0, sub_part, base_b), :]
-    for d in range(1, plane):
-        value = value + slot_b[d - 1]
-    buf[rows(0, sub_part, base_b), :] = value
-    copies = []
-    for d in range(1, pairs):
-        there = (q + d) % pairs
-        copies.append(remote(buf.at[rows(there, piece, base_b)], slot_c.at[d - 1],
-                             cs.at[d - 1], cr.at[d - 1], line_peer(d)))
-        copies[-1].start()
-    for c in copies:
-        c.wait()
-    base_c = base_b + q * piece
-    value = buf[rows(0, piece, base_c), :]
-    for d in range(1, pairs):
-        value = value + slot_c[d - 1]
-    mine = out.at[rows(0, piece, base_c)]
-    out[rows(0, piece, base_c), :] = value
-
-    copies = []
-    for d in range(1, pairs):
-        copies.append(remote(mine, mine, gcs.at[d - 1], gcr.at[d - 1], line_peer(d)))
-        copies[-1].start()
-    for c in copies:
-        c.wait()
-    mine = out.at[rows(0, sub_part, base_b)]
-    copies = []
-    for d in range(1, plane):
-        copies.append(remote(mine, mine, gbs.at[d - 1], gbr.at[d - 1], plane_peer(d)))
-        copies[-1].start()
-    for c in copies:
-        c.wait()
-    mine = out.at[rows(0, part, base_a)]
-    copy = remote(mine, mine, gas.at[0], gar.at[0], core_peer)
-    copy.start()
-    copy.wait()
+                        total.buf[pl.ds((n - numbers[0]) * UNIT, UNIT), :] = value
+
+        @pl.when(edge)
+        def _():
+            last = jnp.where(at > 0, 1, 0).astype(jnp.float32)
+            for n in numbers:
+                k, l = blocks[n]
+                m = l - k
+                value = term(n, k, l)
+                less, ends = (dgram, wgram) if n < len(GRAM) else (dcross, wcross)
+                for i in range(max(0, -m), min(2, 2 - m) + 1):
+                    value = value - less[3 * i + i + m] * ((1.0 - last) if i < k else last)
+                value = value - ends[pl.ds(k * UNIT, UNIT), pl.ds(l * UNIT, UNIT)]
+                total.buf[pl.ds((n - numbers[0]) * UNIT, UNIT), :] = value
+        used, size = len(numbers) * UNIT, total.buf.shape[0]
+        if size > used:
+            total.buf[pl.ds(used, size - used), :] = jnp.zeros((size - used, UNIT), jnp.float32)
+
+    gather(gram, list(range(len(GRAM))))
+    gram.send(0)
+    gather(cross, list(range(len(GRAM), NB)))
+    gram.add(0)
+    gram.send(1)
+    cross.send(0)
+    cross.add(0)
+    gram.add(1)
+    gram.send(2)
+    cross.send(1)
+    gram.add(2)
+    gram.share(2)
+    cross.add(1)
+    cross.send(2)
+    gram.wait()
+    gram.share(1)
+    cross.add(2)
+    cross.share(2)
+    gram.wait()
+    gram.share(0)
+    cross.wait()
+    cross.share(1)
+    gram.wait()
+    cross.wait()
+    cross.share(0)
+    cross.wait()
 
     x_extra.wait_send()
     for c in range(CHUNKS):
@@ -442,15 +494,14 @@
     lead = (LAGS - 1) * DELAY + 1
     last_row = count * devices - lead
     pairs = spans // 2
-    piece = -(-NB * UNIT // (devices * 8)) * 8
-    total = piece * devices
+    pieces = [-(-n * UNIT // (devices * 8)) * 8 for n in (len(GRAM), len(CROSS))]
     dma = pltpu.SemaphoreType.DMA
     f32, bf16 = jnp.float32, jnp.bfloat16
     vmem = pl.BlockSpec(memory_space=pltpu.VMEM)
     sums = pl.pallas_call(
-        functools.partial(sums_kernel, groups, spans, piece),
-        out_shape=jax.ShapeDtypeStruct((total, comps), f32),
-        in_specs=[pl.BlockSpec(memory_space=pl.ANY)], out_specs=vmem,
+        functools.partial(sums_kernel, groups, spans, pieces),
+        out_shape=[jax.ShapeDtypeStruct((piece * devices, comps), f32) for piece in pieces],
+        in_specs=[pl.BlockSpec(memory_space=pl.ANY)], out_specs=[vmem, vmem],
         scratch_shapes=[
             pltpu.VMEM((12, HALF + 8, UNIT), f32),
             pltpu.VMEM((LAGS + 1, DELAY, UNIT), f32),
@@ -465,13 +516,13 @@
             pltpu.VMEM((9, UNIT, UNIT), f32),
             pltpu.VMEM((LAGS * UNIT, LAGS * UNIT), f32),
             pltpu.VMEM((LAGS * UNIT, LAGS * UNIT), f32),
-            pltpu.VMEM((total, UNIT), f32),
-            pltpu.VMEM((total // 2, UNIT), f32),
-            pltpu.VMEM((groups - 1, pairs * piece, UNIT), f32),
-            pltpu.VMEM((pairs - 1, piece, UNIT), f32),
             dma((3,)), dma((CHUNKS,)), dma((CHUNKS,)), dma((CHUNKS,)), dma((CHUNKS,)), dma((3,)), dma((3,)),
-            dma((1,)), dma((1,)), dma((groups - 1,)), dma((groups - 1,)), dma((pairs - 1,)), dma((pairs - 1,)),
-            dma((pairs - 1,)), dma((pairs - 1,)), dma((groups - 1,)), dma((groups - 1,)), dma((1,)), dma((1,)),
+            *(ref for piece in pieces for ref in (
+                pltpu.VMEM((piece * devices, UNIT), f32),
+                pltpu.VMEM((1, piece * devices // 2, UNIT), f32),
+                pltpu.VMEM((groups - 1, pairs * piece, UNIT), f32),
+                pltpu.VMEM((pairs - 1, piece, UNIT), f32),
+                *(dma((3, max(groups, pairs) - 1)),) * 4)),
         ],
         compiler_params=pltpu.CompilerParams(
             collective_id=0, has_side_effects=True, vmem_limit_bytes=56 << 20),
@@ -480,13 +531,13 @@
     return pl.pallas_call(
         functools.partial(solve_kernel, comps, 1.0 / last_row),
         out_shape=(jax.ShapeDtypeStruct((size, size), f32),) * 2,
-        in_specs=[vmem], out_specs=(vmem, vmem),
+        in_specs=[vmem, vmem], out_specs=(vmem, vmem),
         scratch_shapes=[
             pltpu.VMEM((LAGS, comps, 2 * size), f32),
             pltpu.VMEM((LAGS, comps, comps), f32),
         ],
         compiler_params=pltpu.CompilerParams(vmem_limit_bytes=48 << 20),
-    )(sums)
+    )(*sums)
 
 
 def solution(mesh):

time: 135 us -> 114 us (0.84)
  Pallas kernels: 131 us -> 110 us
    pallas_call x1, Pallas kernels: 54.5 us -> 36.9 us  [on_device(): pl.pallas_call(functools.partial(solve_kernel, comps, 1.0 / last_row), ou...]
    pallas_call x1, Pallas kernels: 76.5 us -> 73.4 us  [on_device(): pl.pallas_call(functools.partial(sums_kernel, groups, spans, pieces), out...]
where the time goes in v1:
time: 114 us; the launch traced here: 113 us
  Pallas kernels  110 us (96%)
  local copies, waits for them, and re-layouts  2.3 us (2%)
    pallas_call x1, Pallas kernels, on_device(): pl.pallas_call(functools.partial(sums_kernel, groups, spans, pieces), out...  73.4 us
    pallas_call x1, Pallas kernels, on_device(): pl.pallas_call(functools.partial(solve_kernel, comps, 1.0 / last_row), ou...  36.9 us
    unnamed x4, local copies, waits for them, and re-layouts  2.3 us

profile of v1, /device:TPU:0, one launch (start us, length us, event | category | flops | bytes accessed | tf_op | source)
XLA Modules:
  0.0 113.3 jit_solution(15356282278378251120)
XLA Ops:
  0.6 73.4 %shard_map.30 = (f32[1280,128]{1,0:T(8,128)}, f32[2048,128]{1,0:T(8,128)}) custom-call(f32[4,1024,128]{2,1,0:T(8,128)} %bitcast.1), custom_call_target="tpu_custom_call" | custom-call | tf_op jit(solution)/shard_map/pallas_call | solution.py:501
  74.1 0.0 copy-start
  74.1 1.2 %copy-done = f32[2048,128]{1,0:T(8,128)S(1)} copy-done((f32[2048,128]{1,0:T(8,128)S(1)}, f32[2048,128]{1,0:T(8,128)}, u32[]{:S(2)}) %copy-start) | copy-done | bytes 1048600
  75.3 0.0 copy-start.1
  75.3 1.1 copy-done.1
  76.4 36.9 %shard_map.31 = (f32[512,512]{1,0:T(8,128)}, f32[512,512]{1,0:T(8,128)}) custom-call(f32[1280,128]{1,0:T(8,128)S(1)} %copy-done.1, f32[2048,128]{1,0:T(8,128)S(1)} %copy-done), custom_call_target="tpu_custom_call" | custom-call | tf_op jit(solution)/shard_map/pallas_call | solution.py:531
Async XLA Ops:
  74.1 1.2 %copy-start = (f32[2048,128]{1,0:T(8,128)S(1)}, f32[2048,128]{1,0:T(8,128)}, u32[]{:S(2)}) copy-start(f32[2048,128]{1,0:T(8,128)} %get-tuple-element.5.cross_ref) | copy-start | bytes 3145732
  75.3 1.1 copy-start.1

commit v2 on v1

--- a/solution.py
+++ b/solution.py
@@ -82,46 +82,55 @@
     return jnp.concatenate(a, 0), jnp.concatenate(b, 0)
 
 
-def solve_kernel(comps, scale, gram_ref, cross_ref, tri_ref, op_ref, work, inverses):
-    size = LAGS * comps
-    for i in range(LAGS):
-        rows = pl.ds(i * comps, comps)
-        for j in range(LAGS):
-            if j >= i:
-                at = GRAM.index((i, j)) * comps
-                work[i, :, pl.ds(j * comps, comps)] = gram_ref[pl.ds(at, comps), :] * scale
-            at = CROSS.index((i, j)) * comps
-            work[i, :, pl.ds(size + j * comps, comps)] = cross_ref[pl.ds(at, comps), :] * scale
-        if i:
-            work[i, :, pl.ds(0, i * comps)] = jnp.zeros((comps, i * comps), jnp.float32)
-            tri_ref[rows, pl.ds(0, i * comps)] = jnp.zeros((comps, i * comps), jnp.float32)
-
-    def step(i, carry):
-        at = pl.multiple_of(i * comps, comps)
-        upper, inverse = factor(work[i, :, pl.ds(at, comps)])
-        inverses[i] = inverse
+class Solve:
+    def __init__(self, scale, gram, cross, tri, op, work, mid, inverses):
+        self.scale, self.gram, self.cross, self.tri, self.op = scale, gram, cross, tri, op
+        self.work, self.mid, self.inverses = work, mid, inverses
+
+    def load(self):
+        for i in range(LAGS):
+            for j in range(LAGS):
+                to = pl.ds(j * UNIT, UNIT)
+                if j >= i:
+                    at = GRAM.index((i, j)) * UNIT
+                    self.work[i, :, to] = self.gram[pl.ds(at, UNIT), :] * self.scale
+                else:
+                    self.work[i, :, to] = jnp.zeros((UNIT, UNIT), jnp.float32)
+
+    def step(self, i):
+        work = self.work
+        at = pl.ds(pl.multiple_of(i * UNIT, UNIT), UNIT)
+        upper, inverse = factor(work[i, :, at])
+        self.inverses[i] = inverse
         work[i] = contract(inverse, work[i], ((1,), (0,)), HIGH)
-        work[i, :, pl.ds(at, comps)] = upper
+        work[i, :, at] = upper
 
         def update(j, carry):
-            to = pl.multiple_of(j * comps, comps)
-            work[j] = work[j] - contract(work[i, :, pl.ds(to, comps)], work[i], ((0,), (0,)), HIGH)
+            to = pl.ds(pl.multiple_of(j * UNIT, UNIT), UNIT)
+            work[j] = work[j] - contract(work[i, :, to], work[i], ((0,), (0,)), HIGH)
             return carry
         lax.fori_loop(i + 1, LAGS, update, 0)
-        return carry
-    lax.fori_loop(0, LAGS, step, 0)
-
-    for i in range(LAGS):
-        for j in range(i, LAGS):
-            tri_ref[pl.ds(i * comps, comps), pl.ds(j * comps, comps)] = work[i, :, pl.ds(j * comps, comps)]
-    for b in range(LAGS):
-        rest = jnp.concatenate(
-            [work[i, :, pl.ds((LAGS + b) * comps, comps)] for i in range(LAGS)], 0)
-        if b:
-            rest = rest - contract(
-                op_ref[:, pl.ds(0, b * comps)],
-                tri_ref[pl.ds(0, b * comps), pl.ds(b * comps, comps)], ((1,), (0,)), HIGH)
-        op_ref[:, pl.ds(b * comps, comps)] = contract(rest, inverses[b], ((1,), (1,)), HIGH)
+
+    def finish(self):
+        work, mid, tri, op = self.work, self.mid, self.tri, self.op
+        for i in range(LAGS):
+            rows = pl.ds(i * UNIT, UNIT)
+            tri[rows, pl.ds(i * UNIT, (LAGS - i) * UNIT)] = work[i, :, pl.ds(i * UNIT, (LAGS - i) * UNIT)]
+            if i:
+                tri[rows, pl.ds(0, i * UNIT)] = jnp.zeros((UNIT, i * UNIT), jnp.float32)
+            right = jnp.concatenate(
+                [self.cross[pl.ds(CROSS.index((i, j)) * UNIT, UNIT), :] for j in range(LAGS)], 1) * self.scale
+            if i:
+                over = jnp.concatenate([work[j, :, rows] for j in range(i)], 0)
+                right = right - contract(over, mid[pl.ds(0, i * UNIT), :], ((0,), (0,)), HIGH)
+            mid[rows, :] = contract(self.inverses[i], right, ((1,), (0,)), HIGH)
+        for b in range(LAGS):
+            cols = pl.ds(b * UNIT, UNIT)
+            rest = mid[:, cols]
+            if b:
+                rest = rest - contract(
+                    op[:, pl.ds(0, b * UNIT)], tri[pl.ds(0, b * UNIT), cols], ((1,), (0,)), HIGH)
+            op[:, cols] = contract(rest, self.inverses[b], ((1,), (1,)), HIGH)
 
 
 def halves(x):
@@ -193,20 +202,25 @@
         else:
             self.buf[mine, :] = value
 
-    def share(self, level):
+    def share(self, level, start=True):
         mine = self.out.at[self.rows(level, self.index[level])]
         self.copies = []
         for d in range(1, self.counts[level]):
             self.copies.append(self.remote(
                 mine, mine, self.sems[2].at[level, d - 1], self.sems[3].at[level, d - 1], self.peers[level](d)))
-            self.copies[-1].start()
+        if start:
+            self.start()
+
+    def start(self):
+        for copy in self.copies:
+            copy.start()
 
     def wait(self):
         for copy in self.copies:
             copy.wait()
 
 
-def sums_kernel(groups, spans, pieces, rec, gram_out, cross_out, ext, own, left, right, after, acc,
+def whole_kernel(groups, spans, pieces, scale, rec, tri, op, gram_out, cross_out, work, mid, inverses, ext, own, left, right, after, acc,
                 eleft, eright, eafter, dgram, dcross, wgram, wcross,
                 local_sem, xs, xr, zs, zr, es, er, *reduce_refs):
     grp, span = lax.axis_index("grp"), lax.axis_index("span")
@@ -382,30 +396,44 @@
     def _():
         ext[pl.ds(11, 1), pl.ds(HALF, 8), :] = jnp.zeros((1, 8, UNIT), jnp.float32)
 
-    def chunk(step, carry):
-        c = CHUNKS - 1 - step
+    def load(c):
+        def unit(t, base):
+            e = base + t
+            prepare(ext[e + 1, pl.ds(pl.multiple_of(c * UNIT, UNIT), UNIT + 8), :],
+                    pl.multiple_of(e * UNIT, UNIT), left, right, after)
+            return base
+        lax.fori_loop(0, 4, unit, 7 * h)
         x_copy(c).wait_recv()
 
         @pl.when(gets_z)
         def _():
             z_copy(c).wait_recv()
-
-        def unit(e, carry):
-            prepare(ext[e + 1, pl.ds(pl.multiple_of(c * UNIT, UNIT), UNIT + 8), :],
-                    pl.multiple_of(e * UNIT, UNIT), left, right, after)
+        lax.fori_loop(0, 7, unit, 4 * (1 - h))
+
+    def gram_lags():
+        def lag(p, carry):
+            a = h * (3 - p) * UNIT
+            acc[p] += product(left, a, right, a + p * UNIT, 8 * UNIT)
             return carry
-        lax.fori_loop(0, 11, unit, 0)
-
+        lax.fori_loop(0, LAGS, lag, 0)
+
+    def cross_lags():
         def lag(p, carry):
             a = h * (3 - p) * UNIT
             b = a + p * UNIT
-            acc[p] += product(left, a, right, b, 8 * UNIT)
             acc[LAGS + p] += product(left, a, after, b, 8 * UNIT)
             acc[2 * LAGS + p] += product(left, b, after, a, 8 * UNIT)
             return carry
         lax.fori_loop(0, LAGS, lag, 0)
+
+    def chunk(step, carry):
+        load(CHUNKS - 1 - step)
+        gram_lags()
+        cross_lags()
         return carry
-    lax.fori_loop(0, CHUNKS, chunk, 0)
+    lax.fori_loop(0, CHUNKS - 1, chunk, 0)
+    load(0)
+    gram_lags()
 
     def term(n, k, l):
         if n < len(GRAM):
@@ -447,6 +475,7 @@
 
     gather(gram, list(range(len(GRAM))))
     gram.send(0)
+    cross_lags()
     gather(cross, list(range(len(GRAM), NB)))
     gram.add(0)
     gram.send(1)
@@ -468,9 +497,25 @@
     cross.wait()
     cross.share(1)
     gram.wait()
+
+    solve = Solve(scale, gram_out, cross_out, tri, op, work, mid, inverses)
+    solve.load()
+
+    shared = list(cross.copies)
+    cross.share(0, start=False)
+
+    def step(i, carry):
+        solve.step(i)
+
+        @pl.when(i == 0)
+        def _():
+            for copy in shared:
+                copy.wait()
+            cross.start()
+        return carry
+    lax.fori_loop(0, LAGS, step, 0)
     cross.wait()
-    cross.share(0)
-    cross.wait()
+    solve.finish()
 
     x_extra.wait_send()
     for c in range(CHUNKS):
@@ -498,11 +543,16 @@
     dma = pltpu.SemaphoreType.DMA
     f32, bf16 = jnp.float32, jnp.bfloat16
     vmem = pl.BlockSpec(memory_space=pltpu.VMEM)
-    sums = pl.pallas_call(
-        functools.partial(sums_kernel, groups, spans, pieces),
-        out_shape=[jax.ShapeDtypeStruct((piece * devices, comps), f32) for piece in pieces],
-        in_specs=[pl.BlockSpec(memory_space=pl.ANY)], out_specs=[vmem, vmem],
+    size = LAGS * comps
+    return pl.pallas_call(
+        functools.partial(whole_kernel, groups, spans, pieces, 1.0 / last_row),
+        out_shape=(jax.ShapeDtypeStruct((size, size), f32),) * 2,
+        in_specs=[pl.BlockSpec(memory_space=pl.ANY)], out_specs=(vmem, vmem),
         scratch_shapes=[
+            *(pltpu.VMEM((piece * devices, UNIT), f32) for piece in pieces),
+            pltpu.VMEM((LAGS, UNIT, size), f32),
+            pltpu.VMEM((size, size), f32),
+            pltpu.VMEM((LAGS, UNIT, UNIT), f32),
             pltpu.VMEM((12, HALF + 8, UNIT), f32),
             pltpu.VMEM((LAGS + 1, DELAY, UNIT), f32),
             pltpu.VMEM((2 * UNIT, 11 * UNIT), bf16),
@@ -527,17 +577,6 @@
         compiler_params=pltpu.CompilerParams(
             collective_id=0, has_side_effects=True, vmem_limit_bytes=56 << 20),
     )(record.reshape(LAGS, DELAY, comps))
-    size = LAGS * comps
-    return pl.pallas_call(
-        functools.partial(solve_kernel, comps, 1.0 / last_row),
-        out_shape=(jax.ShapeDtypeStruct((size, size), f32),) * 2,
-        in_specs=[vmem, vmem], out_specs=(vmem, vmem),
-        scratch_shapes=[
-            pltpu.VMEM((LAGS, comps, 2 * size), f32),
-            pltpu.VMEM((LAGS, comps, comps), f32),
-        ],
-        compiler_params=pltpu.CompilerParams(vmem_limit_bytes=48 << 20),
-    )(*sums)
 
 
 def solution(mesh):

time: 114 us -> 107 us (0.939)
  Pallas kernels: 110 us -> 102 us
    pallas_call x2 -> x1, Pallas kernels: 110 us -> 102 us  [on_device(): pl.pallas_call(functools.partial(whole_kernel, groups, spans, pieces, 1.0...]
where the time goes in v2:
time: 107 us; the launch traced here: 106 us
  Pallas kernels  102 us (95%)
  local copies, waits for them, and re-layouts  3.32 us (3%)
    pallas_call x1, Pallas kernels, on_device(): pl.pallas_call(functools.partial(whole_kernel, groups, spans, pieces, 1.0...  102 us
    unnamed x4, local copies, waits for them, and re-layouts  3.32 us

profile of v2, /device:TPU:0, one launch (start us, length us, event | category | flops | bytes accessed | tf_op | source)
XLA Modules:
  0.0 106.4 jit_solution(8977663872506037494)
XLA Ops:
  0.6 102.5 %shard_map.30 = (f32[512,512]{1,0:T(8,128)}, f32[512,512]{1,0:T(8,128)}) custom-call(f32[4,1024,128]{2,1,0:T(8,128)} %bitcast.1), custom_call_target="tpu_custom_call" | custom-call | tf_op jit(solution)/shard_map/pallas_call | solution.py:547
  103.1 0.0 copy-start
  103.1 2.4 %copy.5 = f32[512,512]{1,0:T(8,128)} copy(f32[512,512]{1,0:T(8,128)} %get-tuple-element.4) | data formatting | bytes 2097152
  105.5 0.0 copy-done
  105.5 1.0 copy.6
Async XLA Ops:
  103.1 2.4 %copy-start = (f32[512,512]{1,0:T(8,128)S(1)}, f32[512,512]{1,0:T(8,128)}, u32[]{:S(2)}) copy-start(f32[512,512]{1,0:T(8,128)} %get-tuple-element.5) | copy-start | bytes 3145732

commit v3 on v2

--- a/solution.py
+++ b/solution.py
@@ -83,54 +83,77 @@
 
 
 class Solve:
-    def __init__(self, scale, gram, cross, tri, op, work, mid, inverses):
+    def __init__(self, scale, gram, cross, tri, op, work, mid, inverse):
         self.scale, self.gram, self.cross, self.tri, self.op = scale, gram, cross, tri, op
-        self.work, self.mid, self.inverses = work, mid, inverses
+        self.work, self.mid, self.inverse = work, mid, inverse
 
     def load(self):
+        for n, (i, j) in enumerate(GRAM):
+            self.work[cut(i), cut(j)] = self.gram[cut(n), :] * self.scale
+        self.inverse[...] = jnp.zeros(self.inverse.shape, jnp.float32)
+
+    def load_cross(self):
+        for n, (i, j) in enumerate(CROSS):
+            self.mid[cut(i), cut(j)] = self.cross[cut(n), :] * self.scale
+
+    def step(self, k):
+        work, rest = self.work, LAGS - k - 1
+        upper, inverse = factor(work[cut(k), cut(k)])
+        work[cut(k), cut(k)] = upper
+        self.inverse[cut(k), cut(k)] = inverse
+        if rest:
+            work[cut(k), cut(k + 1, rest)] = contract(
+                inverse, work[cut(k), cut(k + 1, rest)], ((1,), (0,)), HIGH)
+        for j in range(k + 1, LAGS):
+            to = (cut(j), cut(j, LAGS - j))
+            work[to] = work[to] - contract(work[cut(k), cut(j)], work[cut(k), to[1]], ((0,), (0,)), HIGH)
+
+    def invert(self, k):
+        inverse = self.inverse
+        if k:
+            inverse[cut(k), cut(0, k)] = contract(
+                inverse[cut(k), cut(k)], inverse[cut(k), cut(0, k)], ((1,), (0,)), HIGH)
+        if k < LAGS - 1:
+            to = (cut(k + 1, LAGS - k - 1), cut(0, k + 1))
+            inverse[to] = inverse[to] - contract(
+                self.work[cut(k), to[0]], inverse[cut(k), to[1]], ((0,), (0,)), HIGH)
+
+    def apply(self, k):
+        mid = self.mid
+        mid[cut(k), :] = contract(self.inverse[cut(k), cut(k)], mid[cut(k), :], ((1,), (0,)), HIGH)
+        if k < LAGS - 1:
+            below = cut(k + 1, LAGS - k - 1)
+            mid[below, :] = mid[below, :] - contract(
+                self.work[cut(k), below], mid[cut(k), :], ((0,), (0,)), HIGH)
+
+    def operate(self, rows, cols, depth):
+        self.op[rows, cols] = contract(
+            self.mid[rows, cut(0, depth)], self.inverse[cols, cut(0, depth)], ((1,), (1,)), HIGH)
+
+    def triangle(self):
         for i in range(LAGS):
-            for j in range(LAGS):
-                to = pl.ds(j * UNIT, UNIT)
-                if j >= i:
-                    at = GRAM.index((i, j)) * UNIT
-                    self.work[i, :, to] = self.gram[pl.ds(at, UNIT), :] * self.scale
-                else:
-                    self.work[i, :, to] = jnp.zeros((UNIT, UNIT), jnp.float32)
-
-    def step(self, i):
-        work = self.work
-        at = pl.ds(pl.multiple_of(i * UNIT, UNIT), UNIT)
-        upper, inverse = factor(work[i, :, at])
-        self.inverses[i] = inverse
-        work[i] = contract(inverse, work[i], ((1,), (0,)), HIGH)
-        work[i, :, at] = upper
-
-        def update(j, carry):
-            to = pl.ds(pl.multiple_of(j * UNIT, UNIT), UNIT)
-            work[j] = work[j] - contract(work[i, :, to], work[i], ((0,), (0,)), HIGH)
-            return carry
-        lax.fori_loop(i + 1, LAGS, update, 0)
-
-    def finish(self):
-        work, mid, tri, op = self.work, self.mid, self.tri, self.op
-        for i in range(LAGS):
-            rows = pl.ds(i * UNIT, UNIT)
-            tri[rows, pl.ds(i * UNIT, (LAGS - i) * UNIT)] = work[i, :, pl.ds(i * UNIT, (LAGS - i) * UNIT)]
+            self.tri[cut(i), cut(i, LAGS - i)] = self.work[cut(i), cut(i, LAGS - i)]
             if i:
-                tri[rows, pl.ds(0, i * UNIT)] = jnp.zeros((UNIT, i * UNIT), jnp.float32)
-            right = jnp.concatenate(
-                [self.cross[pl.ds(CROSS.index((i, j)) * UNIT, UNIT), :] for j in range(LAGS)], 1) * self.scale
-            if i:
-                over = jnp.concatenate([work[j, :, rows] for j in range(i)], 0)
-                right = right - contract(over, mid[pl.ds(0, i * UNIT), :], ((0,), (0,)), HIGH)
-            mid[rows, :] = contract(self.inverses[i], right, ((1,), (0,)), HIGH)
-        for b in range(LAGS):
-            cols = pl.ds(b * UNIT, UNIT)
-            rest = mid[:, cols]
-            if b:
-                rest = rest - contract(
-                    op[:, pl.ds(0, b * UNIT)], tri[pl.ds(0, b * UNIT), cols], ((1,), (0,)), HIGH)
-            op[:, cols] = contract(rest, self.inverses[b], ((1,), (1,)), HIGH)
+                self.tri[cut(i), cut(0, i)] = jnp.zeros((UNIT, i * UNIT), jnp.float32)
+
+    def second_half(self):
+        self.load_cross()
+        self.step(2)
+        self.apply(0)
+        self.apply(1)
+        self.step(3)
+        self.apply(2)
+        self.invert(2)
+        self.operate(cut(0, 3), cut(0, 3), 3)
+        self.apply(3)
+        self.invert(3)
+        self.operate(cut(0, 3), cut(3), 4)
+        self.operate(cut(3), cut(0, 4), 4)
+        self.triangle()
+
+
+def cut(n, count=1):
+    return pl.ds(n * UNIT, count * UNIT)
 
 
 def halves(x):
@@ -475,10 +498,10 @@
 
     gather(gram, list(range(len(GRAM))))
     gram.send(0)
+    gram.add(0)
+    gram.send(1)
     cross_lags()
     gather(cross, list(range(len(GRAM), NB)))
-    gram.add(0)
-    gram.send(1)
     cross.send(0)
     cross.add(0)
     gram.add(1)
@@ -501,21 +524,14 @@
     solve = Solve(scale, gram_out, cross_out, tri, op, work, mid, inverses)
     solve.load()
 
-    shared = list(cross.copies)
-    cross.share(0, start=False)
-
-    def step(i, carry):
-        solve.step(i)
-
-        @pl.when(i == 0)
-        def _():
-            for copy in shared:
-                copy.wait()
-            cross.start()
-        return carry
-    lax.fori_loop(0, LAGS, step, 0)
+    solve.step(0)
+    solve.invert(0)
     cross.wait()
-    solve.finish()
+    cross.share(0)
+    solve.step(1)
+    solve.invert(1)
+    cross.wait()
+    solve.second_half()
 
     x_extra.wait_send()
     for c in range(CHUNKS):
@@ -550,9 +566,7 @@
         in_specs=[pl.BlockSpec(memory_space=pl.ANY)], out_specs=(vmem, vmem),
         scratch_shapes=[
             *(pltpu.VMEM((piece * devices, UNIT), f32) for piece in pieces),
-            pltpu.VMEM((LAGS, UNIT, size), f32),
-            pltpu.VMEM((size, size), f32),
-            pltpu.VMEM((LAGS, UNIT, UNIT), f32),
+            *(pltpu.VMEM((size, size), f32),) * 3,
             pltpu.VMEM((12, HALF + 8, UNIT), f32),
             pltpu.VMEM((LAGS + 1, DELAY, UNIT), f32),
             pltpu.VMEM((2 * UNIT, 11 * UNIT), bf16),

time: 107 us -> 102 us (0.953)
  Pallas kernels: 102 us -> 98.1 us
    pallas_call x1, Pallas kernels: 102 us -> 98.1 us  [on_device(): pl.pallas_call(functools.partial(whole_kernel, groups, spans, pieces, 1.0...]
where the time goes in v3:
time: 102 us
  Pallas kernels  98.1 us (96%)
  local copies, waits for them, and re-layouts  3.32 us (3%)
    pallas_call x1, Pallas kernels, on_device(): pl.pallas_call(functools.partial(whole_kernel, groups, spans, pieces, 1.0...  98.1 us
    unnamed x4, local copies, waits for them, and re-layouts  3.32 us

profile of v3, /device:TPU:0, one launch (start us, length us, event | category | flops | bytes accessed | tf_op | source)
XLA Modules:
  0.0 102.0 jit_solution(16929840256256854510)
XLA Ops:
  0.6 98.1 %shard_map.30 = (f32[512,512]{1,0:T(8,128)}, f32[512,512]{1,0:T(8,128)}) custom-call(f32[4,1024,128]{2,1,0:T(8,128)} %bitcast.1), custom_call_target="tpu_custom_call" | custom-call | tf_op jit(solution)/shard_map/pallas_call | solution.py:563
  98.7 0.0 copy-start
  98.7 2.4 %copy.5 = f32[512,512]{1,0:T(8,128)} copy(f32[512,512]{1,0:T(8,128)} %get-tuple-element.4) | data formatting | bytes 2097152
  101.1 0.0 copy-done
  101.1 1.0 copy.6
Async XLA Ops:
  98.7 2.4 %copy-start = (f32[512,512]{1,0:T(8,128)S(1)}, f32[512,512]{1,0:T(8,128)}, u32[]{:S(2)}) copy-start(f32[512,512]{1,0:T(8,128)} %get-tuple-element.5) | copy-start | bytes 3145732

commit v4 on v3

--- a/solution.py
+++ b/solution.py
@@ -40,6 +40,12 @@
 
     def line(x, i):
         return jnp.broadcast_to(x[i:i + 1, :], (8, n))
+
+    def total(terms):
+        while len(terms) > 2:
+            terms = [terms[0] + terms[1]] + terms[2:] if len(terms) % 2 else [
+                terms[i] + terms[i + 1] for i in range(0, len(terms), 2)]
+        return terms[0] + terms[1]
 
     def stack(rows):
         value = rows[0]
@@ -68,15 +74,13 @@
         for r in reversed(range(8)):
             left[r] = rows[r] * inverse[r]
             right[r] = lines[r] * inverse[r]
-            for i in range(r + 1, 8):
+            for i in reversed(range(r + 1, 8)):
                 left[r] = left[r] - s[i][r] * left[i]
                 right[r] = right[r] - s[i][r] * right[i]
         for h in range(g + 1, groups):
-            old = a[h]
-            for j in range(8):
-                c = column(old, 8 * g + j)
-                a[h] = a[h] - c * left[j]
-                b[h] = b[h] - c * right[j]
+            c = [column(a[h], 8 * g + j) for j in range(8)]
+            a[h] = a[h] - total([c[j] * left[j] for j in reversed(range(8))])
+            b[h] = b[h] - total([c[j] * right[j] for j in reversed(range(8))])
         a[g] = jnp.where(lane >= sub + 8 * g, stack(rows) * scale, 0.0)
         b[g] = stack(lines) * scale
     return jnp.concatenate(a, 0), jnp.concatenate(b, 0)

time: 102 us -> 98.4 us (0.965)
  Pallas kernels: 98.1 us -> 94.3 us
    pallas_call x1, Pallas kernels: 98.1 us -> 94.3 us  [on_device(): pl.pallas_call(functools.partial(whole_kernel, groups, spans, pieces, 1.0...]
where the time goes in v4:
time: 98.4 us; the launch traced here: 98.3 us
  Pallas kernels  94.3 us (96%)
  local copies, waits for them, and re-layouts  3.32 us (3%)
    pallas_call x1, Pallas kernels, on_device(): pl.pallas_call(functools.partial(whole_kernel, groups, spans, pieces, 1.0...  94.3 us
    unnamed x4, local copies, waits for them, and re-layouts  3.32 us

profile of v4, /device:TPU:0, one launch (start us, length us, event | category | flops | bytes accessed | tf_op | source)
XLA Modules:
  0.0 98.3 jit_solution(16511230591200470201)
XLA Ops:
  0.6 94.3 %shard_map.30 = (f32[512,512]{1,0:T(8,128)}, f32[512,512]{1,0:T(8,128)}) custom-call(f32[4,1024,128]{2,1,0:T(8,128)} %bitcast.1), custom_call_target="tpu_custom_call" | custom-call | tf_op jit(solution)/shard_map/pallas_call | solution.py:567
  94.9 0.0 copy-start
  94.9 2.4 %copy.5 = f32[512,512]{1,0:T(8,128)} copy(f32[512,512]{1,0:T(8,128)} %get-tuple-element.4) | data formatting | bytes 2097152
  97.3 0.0 copy-done
  97.3 1.0 copy.6
Async XLA Ops:
  94.9 2.4 %copy-start = (f32[512,512]{1,0:T(8,128)S(1)}, f32[512,512]{1,0:T(8,128)}, u32[]{:S(2)}) copy-start(f32[512,512]{1,0:T(8,128)} %get-tuple-element.5) | copy-start | bytes 3145732

commit v5 on v4

--- a/solution.py
+++ b/solution.py
@@ -58,31 +58,30 @@
         s = [[line(cols[j], i) for j in range(i + 1)] for i in range(8)]
         rows = [line(a[g], i) for i in range(8)]
         lines = [line(b[g], i) for i in range(8)]
-        inverse = []
+        inverse, outs, others = [], [], []
         for r in range(8):
             inverse.append(1.0 / s[r][r])
-            factors = [s[i][r] * inverse[r] for i in range(r + 1, 8)]
-            for i in range(r + 1, 8):
-                for j in range(r + 1, i + 1):
-                    s[i][j] = s[i][j] - factors[i - r - 1] * s[j][r]
-            for i in range(r + 1, 8):
-                s[i][r] = factors[i - r - 1]
-                rows[i] = rows[i] - s[i][r] * rows[r]
-                lines[i] = lines[i] - s[i][r] * lines[r]
+            outs.append(rows[r])
+            others.append(lines[r])
+            pivot = [s[j][r] for j in range(8)]
+            s[r][r + 1:] = pivot[r + 1:]
+            for i in range(8):
+                if i == r:
+                    continue
+                f = s[i][r] * inverse[r]
+                for j in range(r + 1, i + 1 if i > r else 8):
+                    s[i][j] = s[i][j] - f * pivot[j]
+                rows[i] = rows[i] - f * rows[r]
+                lines[i] = lines[i] - f * lines[r]
         scale = lax.rsqrt(stack([s[r][r] for r in range(8)]))
-        left, right = list(rows), list(lines)
-        for r in reversed(range(8)):
-            left[r] = rows[r] * inverse[r]
-            right[r] = lines[r] * inverse[r]
-            for i in reversed(range(r + 1, 8)):
-                left[r] = left[r] - s[i][r] * left[i]
-                right[r] = right[r] - s[i][r] * right[i]
+        left = [rows[r] * inverse[r] for r in range(8)]
+        right = [lines[r] * inverse[r] for r in range(8)]
         for h in range(g + 1, groups):
             c = [column(a[h], 8 * g + j) for j in range(8)]
             a[h] = a[h] - total([c[j] * left[j] for j in reversed(range(8))])
             b[h] = b[h] - total([c[j] * right[j] for j in reversed(range(8))])
-        a[g] = jnp.where(lane >= sub + 8 * g, stack(rows) * scale, 0.0)
-        b[g] = stack(lines) * scale
+        a[g] = jnp.where(lane >= sub + 8 * g, stack(outs) * scale, 0.0)
+        b[g] = stack(others) * scale
     return jnp.concatenate(a, 0), jnp.concatenate(b, 0)
 
 
@@ -429,20 +428,20 @@
             prepare(ext[e + 1, pl.ds(pl.multiple_of(c * UNIT, UNIT), UNIT + 8), :],
                     pl.multiple_of(e * UNIT, UNIT), left, right, after)
             return base
-        lax.fori_loop(0, 4, unit, 7 * h)
+        lax.fori_loop(0, 4, unit, 7 * h, unroll=True)
         x_copy(c).wait_recv()
 
         @pl.when(gets_z)
         def _():
             z_copy(c).wait_recv()
-        lax.fori_loop(0, 7, unit, 4 * (1 - h))
+        lax.fori_loop(0, 7, unit, 4 * (1 - h), unroll=True)
 
     def gram_lags():
         def lag(p, carry):
             a = h * (3 - p) * UNIT
             acc[p] += product(left, a, right, a + p * UNIT, 8 * UNIT)
             return carry
-        lax.fori_loop(0, LAGS, lag, 0)
+        lax.fori_loop(0, LAGS, lag, 0, unroll=True)
 
     def cross_lags():
         def lag(p, carry):

time: 98.4 us -> 93.9 us (0.954)
  Pallas kernels: 94.3 us -> 89.8 us
    pallas_call x1, Pallas kernels: 94.3 us -> 89.8 us  [on_device(): pl.pallas_call(functools.partial(whole_kernel, groups, spans, pieces, 1.0...]
where the time goes in v5:
time: 93.9 us; the launch traced here: 93.8 us
  Pallas kernels  89.8 us (96%)
  local copies, waits for them, and re-layouts  3.32 us (4%)
    pallas_call x1, Pallas kernels, on_device(): pl.pallas_call(functools.partial(whole_kernel, groups, spans, pieces, 1.0...  89.8 us
    unnamed x4, local copies, waits for them, and re-layouts  3.32 us

profile of v5, /device:TPU:0, one launch (start us, length us, event | category | flops | bytes accessed | tf_op | source)
XLA Modules:
  0.0 93.8 jit_solution(13838778067383819356)
XLA Ops:
  0.6 89.8 %shard_map.30 = (f32[512,512]{1,0:T(8,128)}, f32[512,512]{1,0:T(8,128)}) custom-call(f32[4,1024,128]{2,1,0:T(8,128)} %bitcast.1), custom_call_target="tpu_custom_call" | custom-call | tf_op jit(solution)/shard_map/pallas_call | solution.py:566
  90.4 0.0 copy-start
  90.5 2.4 %copy.5 = f32[512,512]{1,0:T(8,128)} copy(f32[512,512]{1,0:T(8,128)} %get-tuple-element.4) | data formatting | bytes 2097152
  92.8 0.0 copy-done
  92.8 1.0 %copy.6 = f32[512,512]{1,0:T(8,128)} copy(f32[512,512]{1,0:T(8,128)S(1)} %copy-done) | data formatting | bytes 2097152
Async XLA Ops:
  90.4 2.4 %copy-start = (f32[512,512]{1,0:T(8,128)S(1)}, f32[512,512]{1,0:T(8,128)}, u32[]{:S(2)}) copy-start(f32[512,512]{1,0:T(8,128)} %get-tuple-element.5) | copy-start | bytes 3145732

commit v6 on v5

--- a/solution.py
+++ b/solution.py
@@ -450,7 +450,7 @@
             acc[LAGS + p] += product(left, a, after, b, 8 * UNIT)
             acc[2 * LAGS + p] += product(left, b, after, a, 8 * UNIT)
             return carry
-        lax.fori_loop(0, LAGS, lag, 0)
+        lax.fori_loop(0, LAGS, lag, 0, unroll=True)
 
     def chunk(step, carry):
         load(CHUNKS - 1 - step)

time: 93.9 us -> 92 us (0.980)
  Pallas kernels: 89.8 us -> 87.8 us
    pallas_call x1, Pallas kernels: 89.8 us -> 87.8 us  [on_device(): pl.pallas_call(functools.partial(whole_kernel, groups, spans, pieces, 1.0...]
where the time goes in v6:
time: 92 us; the launch traced here: 91.8 us
  Pallas kernels  87.8 us (95%)
  local copies, waits for them, and re-layouts  3.32 us (4%)
    pallas_call x1, Pallas kernels, on_device(): pl.pallas_call(functools.partial(whole_kernel, groups, spans, pieces, 1.0...  87.8 us
    unnamed x4, local copies, waits for them, and re-layouts  3.32 us

profile of v6, /device:TPU:0, one launch (start us, length us, event | category | flops | bytes accessed | tf_op | source)
XLA Modules:
  0.0 91.8 jit_solution(5010165806093139595)
XLA Ops:
  0.6 87.8 %shard_map.30 = (f32[512,512]{1,0:T(8,128)}, f32[512,512]{1,0:T(8,128)}) custom-call(f32[4,1024,128]{2,1,0:T(8,128)} %bitcast.1), custom_call_target="tpu_custom_call" | custom-call | tf_op jit(solution)/shard_map/pallas_call | solution.py:566
  88.5 0.0 copy-start
  88.5 2.4 %copy.5 = f32[512,512]{1,0:T(8,128)} copy(f32[512,512]{1,0:T(8,128)} %get-tuple-element.4) | data formatting | bytes 2097152
  90.8 0.0 copy-done
  90.8 1.0 %copy.6 = f32[512,512]{1,0:T(8,128)} copy(f32[512,512]{1,0:T(8,128)S(1)} %copy-done) | data formatting | bytes 2097152
Async XLA Ops:
  88.5 2.4 %copy-start = (f32[512,512]{1,0:T(8,128)S(1)}, f32[512,512]{1,0:T(8,128)}, u32[]{:S(2)}) copy-start(f32[512,512]{1,0:T(8,128)} %get-tuple-element.5) | copy-start | bytes 3145732
